TPU v7x, 32 devices: a whole 2x2x4 slice. The times are simulated.
32 devices in a mesh: wide: 8 (over z, x), narrow: 4 (over y, core).
Axes of the slice: x: 2, y: 2, z: 4, core: 2. Of those that a mesh axis runs over, the one named last changes fastest.
Arguments:
- block_input: bfloat16 [32, 1024, 768], P(('wide', 'narrow')), may hold values from -6 to 6
- segments: int32 [32, 1024], P(('wide', 'narrow')), may hold values from 0 to 3, never falling along the last dimension, each value on 1 to 512 neighbouring positions
- real_mask: int32 [32, 1024], P(('wide', 'narrow')), may hold values from 0 to 1, as said below
- qkv_weight: bfloat16 [768, 2304], replicated, may hold values from -0.21875 to 0.21875
- attn_out_weight: bfloat16 [768, 768], replicated, may hold values from -1.75 to 1.75
- ffn_in_weight: bfloat16 [768, 3072], replicated, may hold values from -0.21875 to 0.21875
- ffn_bias: float32 [3072], replicated, may hold values from -3 to 3
- ffn_out_weight: bfloat16 [3072, 768], replicated, may hold values from -0.109375 to 0.109375
- first_gain: float32 [768], replicated, may hold values from 0.25 to 1.75
- first_shift: float32 [768], replicated, may hold values from -2 to 2
- second_gain: float32 [768], replicated, may hold values from 0.25 to 1.75
- second_shift: float32 [768], replicated, may hold values from -2 to 2
- adapter_down: bfloat16 [768, 16, 48], P(None, None, 'narrow'), may hold values from -0.21875 to 0.21875
- adapter_up: bfloat16 [16, 48, 768], P(None, 'narrow'), may hold values from -0.875 to 0.875
- joining_query: bfloat16 [768, 768], replicated, may hold values from -0.4375 to 0.4375
- joining_key: bfloat16 [768, 768], replicated, may hold values from -0.21875 to 0.21875
- joining_value: bfloat16 [768, 768], replicated, may hold values from -0.21875 to 0.21875
- cotangent: bfloat16 [32, 1024, 768], P(('wide', 'narrow')), may hold values from -6 to 6
Outputs:
- block_output: bfloat16 [32, 1024, 768], P(('wide', 'narrow'))
- input_grad: bfloat16 [32, 1024, 768], P(('wide', 'narrow'))
- query_grad: float32 [768, 768], replicated
- key_grad: float32 [768, 768], replicated
- value_grad: float32 [768, 768], replicated
- ffn_bias_grad: float32 [3072], replicated
- first_gain_grad: float32 [768], replicated
- first_shift_grad: float32 [768], replicated
- second_gain_grad: float32 [768], replicated
- second_shift_grad: float32 [768], replicated
- entropy: float32 [], replicated
Inputs may be any that keep to these rules, and one draw needn't show every extreme that they name: `segments`: within a row the ids never fall; a row holds at most 4 documents of 1 to 512 tokens, and one of them has exactly 512. `real_mask`: in each row the real tokens form a leading run, and every row has at least one.
All inputs are finite; a program needn't handle non-finite values.
Results may differ from a plain program's by a relative error of at most 0.02.
Values may be sent and summed in bfloat16 or wider, within the bound.
A program may use at most 256 MiB of HBM per device.

v0:
```python
import math

import jax
import jax.numpy as jnp
from jax import lax
from jax.sharding import PartitionSpec as P

D = 768
HEADS = 12
HEAD_DIM = 64
ADAPTERS = 16
BOTTLE = 48


def matmul(left_op, right_op):
    return jnp.dot(left_op, right_op, preferred_element_type=jnp.float32)


def contract_rows(left_op, right_op):
    return lax.dot_general(
        left_op, right_op, (((0,), (0,)), ((), ())), preferred_element_type=jnp.float32
    )


def contract_cols(left_op, right_op):
    return lax.dot_general(
        left_op, right_op, (((1,), (1,)), ((), ())), preferred_element_type=jnp.float32
    )


def normalize(values):
    centre = values - jnp.mean(values, axis=-1, keepdims=True)
    factor = lax.rsqrt(jnp.mean(centre * centre, axis=-1, keepdims=True) + 1e-06)
    return (centre * factor, factor)


def norm_back(grad_out, unit_vals, factor, gain_vec):
    scaled = grad_out * gain_vec
    return factor * (
        scaled
        - jnp.mean(scaled, axis=-1, keepdims=True)
        - unit_vals * jnp.mean(scaled * unit_vals, axis=-1, keepdims=True)
    )


def gelu_slope(values):
    return 0.5 * (1.0 + lax.erf(values * (1.0 / math.sqrt(2.0)))) + values * jnp.exp(
        -0.5 * values * values
    ) * (1.0 / math.sqrt(2.0 * math.pi))


def per_device(
    block_input,
    segments,
    real_mask,
    qkv_weight,
    attn_out_weight,
    ffn_in_weight,
    ffn_bias,
    ffn_out_weight,
    first_gain,
    first_shift,
    second_gain,
    second_shift,
    adapter_down,
    adapter_up,
    joining_query,
    joining_key,
    joining_value,
    cotangent,
):
    row_count, seq_len, width = block_input.shape
    token_count = row_count * seq_len
    blk_size = min(512, seq_len)
    blk_count = seq_len // blk_size
    att_scale = 1.0 / math.sqrt(HEAD_DIM)
    mix_scale = 1.0 / math.sqrt(D)
    bank_width = ADAPTERS * BOTTLE
    down_full, up_full = (
        lax.all_gather(adapter_down, "narrow", axis=2, tiled=True),
        lax.all_gather(adapter_up, "narrow", axis=1, tiled=True),
    )
    down_flat = down_full.reshape(width, bank_width)
    up_flat = up_full.reshape(bank_width, width)

    def split_heads(packed_row):
        head_view = packed_row.reshape(seq_len, 3, HEADS, HEAD_DIM)
        return (head_view[:, 0], head_view[:, 1], head_view[:, 2])

    def block_logits(queries_blk, seg_blk, key_heads, seg_row):
        raw_scores = (
            jnp.einsum("qhd,khd->hqk", queries_blk, key_heads, preferred_element_type=jnp.float32)
            * att_scale
        )
        same_doc = (seg_blk[:, None] == seg_row[None, :])[None]
        return jnp.where(same_doc, raw_scores, -1e30)

    def attend_row(row_item):
        packed_row, seg_row = row_item
        queries, key_heads, value_heads = split_heads(packed_row)

        def block_step(carried, block_index):
            offset = block_index * blk_size
            queries_blk = lax.dynamic_slice_in_dim(queries, offset, blk_size, 0)
            seg_blk = lax.dynamic_slice_in_dim(seg_row, offset, blk_size, 0)
            logits = block_logits(queries_blk, seg_blk, key_heads, seg_row)
            row_top = jnp.max(logits, axis=-1, keepdims=True)
            exp_scores = jnp.exp(logits - row_top)
            row_total = jnp.sum(exp_scores, axis=-1, keepdims=True)
            prob_low = (exp_scores / row_total).astype(jnp.bfloat16)
            context = jnp.einsum(
                "hqk,khd->qhd", prob_low, value_heads, preferred_element_type=jnp.float32
            )
            return (
                carried,
                (context.astype(jnp.bfloat16), (row_top + jnp.log(row_total))[:, :, 0]),
            )

        unused, (context, log_total) = lax.scan(
            block_step, jnp.zeros((), jnp.float32), jnp.arange(blk_count)
        )
        return (
            context.reshape(seq_len, width),
            jnp.transpose(log_total, (1, 0, 2)).reshape(HEADS, seq_len),
        )

    def attend_back(row_item):
        packed_row, seg_row, log_total, grad_row = row_item
        queries, key_heads, value_heads = split_heads(packed_row)
        queries_wide = queries.astype(jnp.float32)
        keys_wide = key_heads.astype(jnp.float32)
        grad_heads = grad_row.reshape(seq_len, HEADS, HEAD_DIM)

        def block_step(carried, block_index):
            grad_keys, grad_values = carried
            offset = block_index * blk_size
            queries_blk = lax.dynamic_slice_in_dim(queries, offset, blk_size, 0)
            queries_blk_wide = lax.dynamic_slice_in_dim(queries_wide, offset, blk_size, 0)
            seg_blk = lax.dynamic_slice_in_dim(seg_row, offset, blk_size, 0)
            grad_blk = lax.dynamic_slice_in_dim(grad_heads, offset, blk_size, 0)
            total_blk = lax.dynamic_slice_in_dim(log_total, offset, blk_size, 1)
            logits = block_logits(queries_blk, seg_blk, key_heads, seg_row)
            probs_blk = jnp.exp(logits - total_blk[:, :, None])
            prob_low = probs_blk.astype(jnp.bfloat16)
            grad_probs = jnp.einsum(
                "qhd,khd->hqk", grad_blk, value_heads, preferred_element_type=jnp.float32
            )
            inner_sum = jnp.sum(grad_probs * probs_blk, axis=-1, keepdims=True)
            grad_logits = probs_blk * (grad_probs - inner_sum)
            grad_queries = (
                jnp.einsum(
                    "hqk,khd->qhd",
                    grad_logits,
                    keys_wide,
                    precision=lax.Precision.HIGHEST,
                    preferred_element_type=jnp.float32,
                )
                * att_scale
            )
            grad_keys = (
                grad_keys
                + jnp.einsum(
                    "hqk,qhd->khd",
                    grad_logits,
                    queries_blk_wide,
                    precision=lax.Precision.HIGHEST,
                    preferred_element_type=jnp.float32,
                )
                * att_scale
            )
            grad_values = grad_values + jnp.einsum(
                "hqk,qhd->khd", prob_low, grad_blk, preferred_element_type=jnp.float32
            )
            return ((grad_keys, grad_values), grad_queries.astype(jnp.bfloat16))

        zero_heads = jnp.zeros((seq_len, HEADS, HEAD_DIM), jnp.float32)
        (grad_keys, grad_values), grad_queries = lax.scan(
            block_step, (zero_heads, zero_heads), jnp.arange(blk_count)
        )
        grad_queries = grad_queries.reshape(seq_len, HEADS, HEAD_DIM)
        stacked = jnp.stack(
            [grad_queries, grad_keys.astype(jnp.bfloat16), grad_values.astype(jnp.bfloat16)], axis=1
        )
        return stacked.reshape(seq_len, 3 * width)

    tokens = block_input.reshape(token_count, width)
    packed = matmul(tokens, qkv_weight).astype(jnp.bfloat16)
    packed_rows = packed.reshape(row_count, seq_len, 3 * width)
    context, log_total = lax.map(attend_row, (packed_rows, segments))
    context = context.reshape(token_count, width)
    attn_out = matmul(context, attn_out_weight)
    unit_one, factor_one = normalize(tokens.astype(jnp.float32) + attn_out)
    h_one = unit_one * first_gain + first_shift
    ffn_pre = matmul(h_one.astype(jnp.bfloat16), ffn_in_weight) + ffn_bias
    act_low = jax.nn.gelu(ffn_pre, approximate=False).astype(jnp.bfloat16)
    ffn_out = matmul(act_low, ffn_out_weight)
    unit_two, factor_two = normalize(h_one + ffn_out)
    h_two = unit_two * second_gain + second_shift
    h_low = h_two.astype(jnp.bfloat16)
    query_low = matmul(h_low, joining_query).astype(jnp.bfloat16)
    probe_low = contract_cols(query_low, joining_key).astype(jnp.bfloat16)
    down_pre = matmul(h_low, down_flat)
    bottle = jax.nn.gelu(down_pre, approximate=False).reshape(token_count, ADAPTERS, BOTTLE)
    guide = contract_cols(probe_low, up_flat).reshape(token_count, ADAPTERS, BOTTLE)
    scores = jnp.sum(bottle * guide, axis=-1) * mix_scale
    shifted = scores - jnp.max(scores, axis=-1, keepdims=True)
    log_weights = shifted - jnp.log(jnp.sum(jnp.exp(shifted), axis=-1, keepdims=True))
    mix_weights = jnp.exp(log_weights)
    mixed_low = (
        (mix_weights[:, :, None] * bottle).reshape(token_count, bank_width).astype(jnp.bfloat16)
    )
    update = matmul(mixed_low, up_flat)
    blend_low = (h_two + update).astype(jnp.bfloat16)
    block_output = (h_two + matmul(blend_low, joining_value)).astype(jnp.bfloat16)
    real_rows = real_mask.reshape(token_count).astype(jnp.float32)
    ent_local = jnp.sum(-jnp.sum(mix_weights * log_weights, axis=-1) * real_rows)
    count_local = jnp.sum(real_rows)
    ent_total = lax.psum(ent_local, ("wide", "narrow"))
    grad_out = cotangent.reshape(token_count, width)
    value_grad = contract_rows(blend_low, grad_out)
    grad_blend = contract_cols(grad_out, joining_value)
    grad_update = grad_blend.astype(jnp.bfloat16)
    grad_mixed = contract_cols(grad_update, up_flat).reshape(token_count, ADAPTERS, BOTTLE)
    grad_weights = jnp.sum(grad_mixed * bottle, axis=-1)
    grad_scores = mix_weights * (
        grad_weights - jnp.sum(grad_weights * mix_weights, axis=-1, keepdims=True)
    )
    score_term = (grad_scores * mix_scale)[:, :, None]
    grad_guide = (score_term * bottle).reshape(token_count, bank_width)
    grad_bottle = (grad_mixed * mix_weights[:, :, None] + score_term * guide).reshape(
        token_count, bank_width
    )
    grad_down = grad_bottle * gelu_slope(down_pre)
    up_wide = up_flat.astype(jnp.float32)
    down_wide = down_flat.astype(jnp.float32)
    grad_probe = jnp.dot(
        grad_guide, up_wide, precision=lax.Precision.HIGHEST, preferred_element_type=jnp.float32
    ).astype(jnp.bfloat16)
    key_grad = contract_rows(grad_probe, query_low)
    grad_query = matmul(grad_probe, joining_key).astype(jnp.bfloat16)
    query_grad = contract_rows(h_low, grad_query)
    adapter_back = lax.dot_general(
        grad_down,
        down_wide,
        (((1,), (1,)), ((), ())),
        precision=lax.Precision.HIGHEST,
        preferred_element_type=jnp.float32,
    )
    grad_h_two = (
        grad_out.astype(jnp.float32)
        + grad_blend
        + adapter_back
        + contract_cols(grad_query, joining_query)
    )
    gain_two_grad = jnp.sum(grad_h_two * unit_two, axis=0)
    shift_two_grad = jnp.sum(grad_h_two, axis=0)
    grad_r_two = norm_back(grad_h_two, unit_two, factor_two, second_gain)
    grad_ffn = grad_r_two.astype(jnp.bfloat16)
    grad_pre = (contract_cols(grad_ffn, ffn_out_weight) * gelu_slope(ffn_pre)).astype(jnp.bfloat16)
    bias_grad = jnp.sum(grad_pre.astype(jnp.float32), axis=0)
    grad_h_one = grad_r_two + contract_cols(grad_pre, ffn_in_weight)
    gain_one_grad = jnp.sum(grad_h_one * unit_one, axis=0)
    shift_one_grad = jnp.sum(grad_h_one, axis=0)
    grad_r_one = norm_back(grad_h_one, unit_one, factor_one, first_gain)
    grad_attn = grad_r_one.astype(jnp.bfloat16)
    grad_context = contract_cols(grad_attn, attn_out_weight).astype(jnp.bfloat16)
    grad_packed = lax.map(
        attend_back,
        (packed_rows, segments, log_total, grad_context.reshape(row_count, seq_len, width)),
    )
    grad_packed = grad_packed.reshape(token_count, 3 * width)
    input_grad = (grad_r_one + contract_cols(grad_packed, qkv_weight)).astype(jnp.bfloat16)
    summed_all = lax.psum(
        (
            query_grad,
            key_grad,
            value_grad,
            bias_grad,
            gain_one_grad,
            shift_one_grad,
            gain_two_grad,
            shift_two_grad,
            count_local,
        ),
        ("wide", "narrow"),
    )
    summed = summed_all[:8]
    count_total = summed_all[8]
    entropy = ent_total / count_total
    return (
        block_output.reshape(row_count, seq_len, width),
        input_grad.reshape(row_count, seq_len, width),
        summed[0],
        summed[1],
        summed[2],
        summed[3],
        summed[4],
        summed[5],
        summed[6],
        summed[7],
        entropy,
    )


def solution(mesh):
    placed = (
        P(("wide", "narrow"), None, None),
        P(("wide", "narrow"), None),
        P(("wide", "narrow"), None),
        P(),
        P(),
        P(),
        P(),
        P(),
        P(),
        P(),
        P(),
        P(),
        P(None, None, "narrow"),
        P(None, "narrow", None),
        P(),
        P(),
        P(),
        P(("wide", "narrow"), None, None),
    )
    return jax.shard_map(
        per_device,
        mesh=mesh,
        in_specs=placed,
        out_specs=(
            P(("wide", "narrow"), None, None),
            P(("wide", "narrow"), None, None),
            P(),
            P(),
            P(),
            P(),
            P(),
            P(),
            P(),
            P(),
            P(),
        ),
        check_vma=False,
    )
```

profile of v0, /device:TPU:0, one launch (start us, length us, event | category | flops | bytes accessed | tf_op | source)
XLA Modules:
  0.0 614.3 jit_solution(18191007570231653971)
XLA Ops:
  16.5 4.9 fusion.89
  21.4 3.5 copy.90
  24.9 7.3 %convolution_convert_fusion = bf16[1024,2304]{1,0:T(8,128)(2,1)} fusion(bf16[768,2304]{1,0:T(8,128)(2,1)S(1)} %copy-done, bf16[1,1024,768]{2,1,0:T(8,128)(2,1)} %param.22), kind=kOutput, calls=%fused_computation.75 | convolution fusion | flops 3626237952 | bytes 9830400 | tf_op jit(solution)/shard_map/dot_general | solution.py:16
  32.2 6.7 %copy.82 = bf16[1024,2304]{0,1:T(8,128)(2,1)} copy(bf16[1024,2304]{1,0:T(8,128)(2,1)} %convolution_convert_fusion) | data formatting | bytes 9437184 | tf_op jit(solution)/shard_map/convert_element_type | solution.py:187
  38.9 6.9 %fusion.147 = (f32[1024,12,64]{0,2,1:T(8,128)}, f32[1024,12,64]{0,2,1:T(8,128)}, bf16[1024,12,64]{0,2,1:T(8,128)(2,1)}, bf16[1024,12,64]{0,2,1:T(8,128)(2,1)}, bf16[1024,12,64]{0,2,1:T(8,128)(2,1)}) fusion(bf16[1024,3,12,64]{0,3,2,1:T(8,128)(2,1)} %bitcast.146), kind=kLoop, calls=%fused_computation.224 | loop fusion | flops 1572864 | bytes 15728640 | tf_op jit(solution)/shard_map/while/body/eval_jaxpr/convert_element_type | solution.py:131
  47.1 81.4 %while.45 = (s32[]{:T(128)}, bf16[2,512,12,64]{1,3,2,0:T(8,128)(2,1)}, f32[2,12,512]{2,1,0:T(8,128)}, s32[2]{0:T(128)S(1)}, s32[1024]{0:T(1024)S(1)}, /*index=5*...) while((s32[]{:T(128)}, ...), condition=%wide.region_3.4_spmd, body=%wide.region_0.3_spmd.sunk | while | flops 1687021568 | bytes 189892912 | solution.py:119
  49.0 14.4 %fusion.208 = (f32[12,512]{1,0:T(8,128)S(1)}, f32[12,512,1024]{2,1,0:T(8,128)}) fusion(pred[512,1024]{1,0:T(8,128)(4,1)S(1)} %broadcast_compare_fusion.4, bf16[1024,12,64]{0,2,1:T(8,128)(2,1)} %get-tuple-element.501, bf16[1024,12,64]{0,2,1:T(8,128)(2,1)} %get-tuple-element.500, s32[]{:T(128)S(6)} %select_n.68), kind=kOutput, calls=%fused_computation.3.clone.1 | convolution fusion | flops 824174592 | bytes 28073988 | tf_op jit(solution)/shard_map/while/body/eval_jaxpr/while/body/eval_jaxpr/qhd,khd->hqk/dot_general | solution.py:92
  63.4 12.3 %fusion.209 = f32[12,512]{1,0:T(8,128)S(1)} fusion(f32[12,512,1024]{2,1,0:T(8,128)} %get-tuple-element.454, f32[12,512]{1,0:T(8,128)S(1)} %get-tuple-element.455, pred[512,1024]{1,0:T(8,128)(4,1)S(1)} %broadcast_compare_fusion.4), kind=kLoop, calls=%fused_computation.4.clone.1 | loop fusion | flops 25159680 | bytes 25739264 | tf_op jit(solution)/shard_map/while/body/eval_jaxpr/while/body/eval_jaxpr/reduce_sum | solution.py:109
  75.7 3.1 copy-done.1
  78.8 8.5 %fusion.210 = bf16[2,512,12,64]{1,3,2,0:T(8,128)(2,1)} fusion(bf16[2,512,12,64]{1,3,2,0:T(8,128)(2,1)} %get-tuple-element.484, s32[]{:T(128)S(6)} %copy.123, bf16[1024,12,64]{0,2,1:T(8,128)(2,1)S(1)} %copy-done.3, f32[12,512,1024]{2,1,0:T(8,128)S(1)} %copy-done.1, f32[12,512]{1,0:T(8,128)S(1)} %fusion.209, f32[12,512]{1,0:T(8,128)S(1)} %get-tuple-element.455, ...), kind=kOutput, calls=%fused_computation.8.clone.1 | convolution fusion | flops 837156864 | bytes 28098564 | tf_op jit(solution)/shard_map/while/body/eval_jaxpr/while/body/eval_jaxpr/hqk,khd->qhd/dot_general | solution.py:111
  89.6 14.4 %fusion.208 = (f32[12,512]{1,0:T(8,128)S(1)}, f32[12,512,1024]{2,1,0:T(8,128)}) fusion(pred[512,1024]{1,0:T(8,128)(4,1)S(1)} %broadcast_compare_fusion.4, bf16[1024,12,64]{0,2,1:T(8,128)(2,1)} %get-tuple-element.501, bf16[1024,12,64]{0,2,1:T(8,128)(2,1)} %get-tuple-element.500, s32[]{:T(128)S(6)} %select_n.68), kind=kOutput, calls=%fused_computation.3.clone.1 | convolution fusion | flops 824174592 | bytes 28073988 | tf_op jit(solution)/shard_map/while/body/eval_jaxpr/while/body/eval_jaxpr/qhd,khd->hqk/dot_general | solution.py:92
  104.0 12.3 %fusion.209 = f32[12,512]{1,0:T(8,128)S(1)} fusion(f32[12,512,1024]{2,1,0:T(8,128)} %get-tuple-element.454, f32[12,512]{1,0:T(8,128)S(1)} %get-tuple-element.455, pred[512,1024]{1,0:T(8,128)(4,1)S(1)} %broadcast_compare_fusion.4), kind=kLoop, calls=%fused_computation.4.clone.1 | loop fusion | flops 25159680 | bytes 25739264 | tf_op jit(solution)/shard_map/while/body/eval_jaxpr/while/body/eval_jaxpr/reduce_sum | solution.py:109
  116.3 3.1 copy-done.1
  119.4 8.5 %fusion.210 = bf16[2,512,12,64]{1,3,2,0:T(8,128)(2,1)} fusion(bf16[2,512,12,64]{1,3,2,0:T(8,128)(2,1)} %get-tuple-element.484, s32[]{:T(128)S(6)} %copy.123, bf16[1024,12,64]{0,2,1:T(8,128)(2,1)S(1)} %copy-done.3, f32[12,512,1024]{2,1,0:T(8,128)S(1)} %copy-done.1, f32[12,512]{1,0:T(8,128)S(1)} %fusion.209, f32[12,512]{1,0:T(8,128)S(1)} %get-tuple-element.455, ...), kind=kOutput, calls=%fused_computation.8.clone.1 | convolution fusion | flops 837156864 | bytes 28098564 | tf_op jit(solution)/shard_map/while/body/eval_jaxpr/while/body/eval_jaxpr/hqk,khd->qhd/dot_general | solution.py:111
  130.0 3.2 copy.83
  136.2 8.6 %fusion.85 = f32[1024,3072]{1,0:T(8,128)} fusion(bf16[768,3072]{1,0:T(8,128)(2,1)S(1)} %bitcast.154, f32[1024,768]{0,1:T(8,128)S(1)} %get-tuple-element.323, f32[768]{0:T(1024)S(1)} %copy-done.33, f32[768]{0:T(1024)S(1)} %copy-done.34, f32[1024]{0:T(1024)S(1)} %add_rsqrt_fusion.1, f32[1024]{0:T(1024)S(1)} %broadcast_multiply_fusion.5), kind=kOutput, calls=%fused_computation.141 | convolution fusion | flops 4835770368 | bytes 20461568 | tf_op jit(solution)/shard_map/dot_general | solution.py:16
  144.8 34.7 %fusion.152 = (f32[1024]{0:T(1024)S(1)}, f32[1024,768]{0,1:T(8,128)S(1)}) fusion(bf16[3072,768]{1,0:T(8,128)(2,1)S(1)} %bitcast.168, f32[1024,3072]{1,0:T(8,128)} %fusion.85, f32[3072]{0:T(1024)S(1)} %copy-done.56, f32[768]{0:T(1024)S(1)} %copy-done.33, f32[768]{0:T(1024)S(1)} %copy-done.34, f32[1024]{0:T(1024)S(1)} %add_rsqrt_fusion.1, ...), kind=kOutput, calls=%fused_computation.229 | convolution fusion | flops 5044173824 | bytes 23623680 | tf_op jit(solution)/shard_map/dot_general | solution.py:16
  182.3 2.6 convolution_convert_fusion.4
  187.5 10.5 %fusion.56 = (f32[1024,768]{0,1:T(8,128)}, f32[1024,768]{0,1:T(8,128)}) fusion(bf16[768,768]{0,1:T(8,128)(2,1)S(1)} %bitcast.158, bf16[1024,768]{0,1:T(8,128)(2,1)} %copy-done.21), kind=kOutput, calls=%fused_computation.80 | convolution fusion | flops 1258291200 | bytes 9043968 | tf_op jit(solution)/shard_map/dot_general | solution.py:16
  198.1 7.2 %fusion.94 = f32[1024,16,48]{0,2,1:T(8,128)} fusion(bf16[1024,768]{1,0:T(8,128)(2,1)} %convolution_convert_fusion.4, bf16[768,768]{1,0:T(8,128)(2,1)} %param.37, bf16[16,48,768]{2,0,1:T(8,128)(2,1)} %all-gather.5.cloned.1.call-done), kind=kOutput, calls=%fused_computation.152 | convolution fusion | flops 2416705536 | bytes 7077888 | tf_op jit(solution)/shard_map/dot_general | solution.py:26
  205.2 5.9 multiply_reduce_fusion.5
  211.9 4.5 bitcast_convert_fusion
  216.4 2.8 fusion.154
  223.9 2.8 fusion.153
  226.8 5.1 fusion.62
  232.0 4.4 multiply_reduce_fusion.1
  236.4 15.1 %convert_reduce_fusion = (f32[3072]{0:T(1024)}, bf16[1024,3072]{1,0:T(8,128)(2,1)}) fusion(f32[1024,3072]{1,0:T(8,128)S(1)} %bitcast.150, f32[3072]{0:T(1024)S(1)} %copy-done.57, bf16[3072,768]{1,0:T(8,128)(2,1)} %param.29, f32[1024]{0:T(1024)S(1)} %get-tuple-element.333, f32[1024,768]{0,1:T(8,128)S(1)} %copy-done.5, ...), kind=kOutput, calls=%fused_computation.58 | convolution fusion | flops 4879021056 | bytes 29928448 | tf_op jit(solution)/shard_map/dot_general | solution.py:26
  251.5 12.4 %multiply_reduce_fusion.2 = (f32[768]{0:T(1024)}, f32[1024]{0:T(1024)S(1)}, f32[1024]{0:T(1024)S(1)}, f32[768]{0:T(1024)}, f32[1024,768]{0,1:T(8,128)}) fusion(f32[1024,768]{0,1:T(8,128)S(1)} %copy-done.10, f32[1024]{0:T(1024)S(1)} %add_rsqrt_fusion.1, f32[1024]{0:T(1024)S(1)} %broadcast_multiply_fusion.5, f32[768]{0:T(1024)S(1)} %copy-done.34, ...), kind=kOutput, calls=%fused_computation.91 | convolution fusion | flops 4845203456 | bytes 23638016 | tf_op jit(solution)/shard_map/dot_general | solution.py:26
  268.4 2.8 fusion.87
  271.3 6.0 convolution_convert_fusion.1
  279.1 243.5 %while.46 = (s32[]{:T(128)}, f32[1024,12,64]{0,2,1:T(8,128)}, f32[1024,12,64]{0,2,1:T(8,128)}, bf16[2,512,12,64]{1,3,2,0:T(8,128)(2,1)}, s32[2]{0:T(128)}, /*ind...) while((s32[]{:T(128)}, f32[1024,12,64]{0,2,1:T(8,128)}, ...), condition=%wide.region_19.20_spmd.clone, body=%wide.region_17.19_spmd.clone.sunk | while | flops 12204369920 | bytes 236308816 | solution.py:177
  283.4 14.2 %fusion.218 = f32[12,512,1024]{2,1,0:T(8,128)} fusion(bf16[1024,12,64]{0,2,1:T(8,128)(2,1)} %get-tuple-element.549, bf16[1024,12,64]{0,2,1:T(8,128)(2,1)} %get-tuple-element.548, s32[]{:T(128)S(6)} %select_n.73), kind=kOutput, calls=%fused_computation.31.clone.1 | convolution fusion | flops 805306368 | bytes 27525124 | tf_op jit(solution)/shard_map/while/body/eval_jaxpr/while/body/eval_jaxpr/qhd,khd->hqk/dot_general | solution.py:92
  297.7 13.7 %bitcast_add_fusion.5 = f32[1024,12,64]{0,2,1:T(8,128)} fusion(f32[1024,12,64]{0,2,1:T(8,128)} %get-tuple-element.526, f32[12,512,1024]{2,1,0:T(8,128)} %fusion.218, f32[12,512]{1,0:T(8,128)S(1)} %constant_dynamic-slice_fusion.2, pred[512,1024]{1,0:T(8,128)(4,1)S(1)} %broadcast_compare_fusion.5, pred[]{:T(512)S(6)} %compare.3, ...), kind=kOutput, calls=%fused_computation.24.clone.1 | convolution fusion | flops 832045056 | bytes 32800772 | tf_op jit(solution)/shard_map/while/body/eval_jaxpr/while/body/eval_jaxpr/hqk,qhd->khd/dot_general | solution.py:171
  311.4 19.0 %multiply_reduce_fusion.16 = (f32[12,512]{1,0:T(8,128)}, f32[12,512,1024]{2,1,0:T(8,128)}) fusion(f32[12,512,1024]{2,1,0:T(8,128)} %fusion.218, f32[12,512]{1,0:T(8,128)} %copy-done.8, pred[512,1024]{1,0:T(8,128)(4,1)} %copy-done.2, bf16[1024,12,64]{0,2,1:T(8,128)(2,1)} %get-tuple-element.552, bf16[1024,12,64]{0,2,1:T(8,128)(2,1)} %get-tuple-element.551, ...), kind=kOutput, calls=%fused_computation.17.clone.1 | convolution fusion | flops 836757504 | bytes 53272580 | tf_op jit(solution)/shard_map/while/body/eval_jaxpr/while/body/eval_jaxpr/qhd,khd->hqk/dot_general | solution.py:145
  330.4 40.8 %fusion.219 = bf16[2,512,12,64]{1,3,2,0:T(8,128)(2,1)} fusion(bf16[2,512,12,64]{1,3,2,0:T(8,128)(2,1)} %get-tuple-element.527, s32[]{:T(128)S(6)} %copy.133, f32[1024,12,64]{0,2,1:T(8,128)} %get-tuple-element.553, f32[12,512,1024]{2,1,0:T(8,128)} %get-tuple-element.469, f32[12,512,1024]{2,1,0:T(8,128)} %fusion.218, ...), kind=kOutput, calls=%fused_computation.29.clone.1 | convolution fusion | flops 4864081920 | bytes 54853636 | tf_op jit(solution)/shard_map/while/body/eval_jaxpr/while/body/eval_jaxpr/hqk,khd->qhd/dot_general | solution.py:151
  371.2 29.7 %bitcast_add_fusion.4 = f32[1024,12,64]{0,2,1:T(8,128)} fusion(f32[1024,12,64]{0,2,1:T(8,128)} %get-tuple-element.525, f32[12,512,1024]{2,1,0:T(8,128)} %get-tuple-element.469, f32[12,512,1024]{2,1,0:T(8,128)} %fusion.218, f32[12,512]{1,0:T(8,128)} %get-tuple-element.470, f32[12,512]{1,0:T(8,128)} %copy-done.8, pred[512,1024]{1,0:T(8,128)(4,1)} %copy-done.2, ...), kind=kOutput, calls=%fused_computation.25.clone.1 | convolution fusion | flops 4865654784 | bytes 58785796 | tf_op jit(solution)/shard_map/while/body/eval_jaxpr/while/body/eval_jaxpr/hqk,qhd->khd/dot_general | solution.py:162
  404.1 14.3 %fusion.218 = f32[12,512,1024]{2,1,0:T(8,128)} fusion(bf16[1024,12,64]{0,2,1:T(8,128)(2,1)} %get-tuple-element.549, bf16[1024,12,64]{0,2,1:T(8,128)(2,1)} %get-tuple-element.548, s32[]{:T(128)S(6)} %select_n.73), kind=kOutput, calls=%fused_computation.31.clone.1 | convolution fusion | flops 805306368 | bytes 27525124 | tf_op jit(solution)/shard_map/while/body/eval_jaxpr/while/body/eval_jaxpr/qhd,khd->hqk/dot_general | solution.py:92
  418.5 14.6 %bitcast_add_fusion.5 = f32[1024,12,64]{0,2,1:T(8,128)} fusion(f32[1024,12,64]{0,2,1:T(8,128)} %get-tuple-element.526, f32[12,512,1024]{2,1,0:T(8,128)} %fusion.218, f32[12,512]{1,0:T(8,128)S(1)} %constant_dynamic-slice_fusion.2, pred[512,1024]{1,0:T(8,128)(4,1)S(1)} %broadcast_compare_fusion.5, pred[]{:T(512)S(6)} %compare.3, ...), kind=kOutput, calls=%fused_computation.24.clone.1 | convolution fusion | flops 832045056 | bytes 32800772 | tf_op jit(solution)/shard_map/while/body/eval_jaxpr/while/body/eval_jaxpr/hqk,qhd->khd/dot_general | solution.py:171
  433.1 18.8 %multiply_reduce_fusion.16 = (f32[12,512]{1,0:T(8,128)}, f32[12,512,1024]{2,1,0:T(8,128)}) fusion(f32[12,512,1024]{2,1,0:T(8,128)} %fusion.218, f32[12,512]{1,0:T(8,128)} %copy-done.8, pred[512,1024]{1,0:T(8,128)(4,1)} %copy-done.2, bf16[1024,12,64]{0,2,1:T(8,128)(2,1)} %get-tuple-element.552, bf16[1024,12,64]{0,2,1:T(8,128)(2,1)} %get-tuple-element.551, ...), kind=kOutput, calls=%fused_computation.17.clone.1 | convolution fusion | flops 836757504 | bytes 53272580 | tf_op jit(solution)/shard_map/while/body/eval_jaxpr/while/body/eval_jaxpr/qhd,khd->hqk/dot_general | solution.py:145
  451.9 40.6 %fusion.219 = bf16[2,512,12,64]{1,3,2,0:T(8,128)(2,1)} fusion(bf16[2,512,12,64]{1,3,2,0:T(8,128)(2,1)} %get-tuple-element.527, s32[]{:T(128)S(6)} %copy.133, f32[1024,12,64]{0,2,1:T(8,128)} %get-tuple-element.553, f32[12,512,1024]{2,1,0:T(8,128)} %get-tuple-element.469, f32[12,512,1024]{2,1,0:T(8,128)} %fusion.218, ...), kind=kOutput, calls=%fused_computation.29.clone.1 | convolution fusion | flops 4864081920 | bytes 54853636 | tf_op jit(solution)/shard_map/while/body/eval_jaxpr/while/body/eval_jaxpr/hqk,khd->qhd/dot_general | solution.py:151
  492.5 30.0 %bitcast_add_fusion.4 = f32[1024,12,64]{0,2,1:T(8,128)} fusion(f32[1024,12,64]{0,2,1:T(8,128)} %get-tuple-element.525, f32[12,512,1024]{2,1,0:T(8,128)} %get-tuple-element.469, f32[12,512,1024]{2,1,0:T(8,128)} %fusion.218, f32[12,512]{1,0:T(8,128)} %get-tuple-element.470, f32[12,512]{1,0:T(8,128)} %copy-done.8, pred[512,1024]{1,0:T(8,128)(4,1)} %copy-done.2, ...), kind=kOutput, calls=%fused_computation.25.clone.1 | convolution fusion | flops 4865654784 | bytes 58785796 | tf_op jit(solution)/shard_map/while/body/eval_jaxpr/while/body/eval_jaxpr/hqk,qhd->khd/dot_general | solution.py:162
  522.7 5.7 fusion.110
  530.9 4.2 copy.97
  535.1 3.8 reshape.323
  546.2 5.4 fusion.109
  551.7 2.6 copy.100
  554.9 42.9 %all-reduce = (f32[3072]{0:T(1024)}, f32[768]{0:T(1024)}, f32[768]{0:T(1024)}, f32[768]{0:T(1024)}, f32[768]{0:T(1024)}, /*index=5*/f32[]{:T(128)}, f32[]{:T(128)}) all-reduce(f32[3072]{0:T(1024)} %get-tuple-element.331, f32[768]{0:T(1024)} %get-tuple-element.249, ...), channel_id=1, replica_groups=mesh['wide'=8,'narrow'=4] {'wide','narrow'}, use_global_device_ids=true, to_apply=%region_24.25 | all-reduce | flops 6146 | bytes 49168 | tf_op jit(solution)/shard_map/psum | solution.py:273
  599.2 3.4 copy.144
  (222 shorter events, 54.9 us)
Async XLA Ops:
  7.2 17.7 %copy-start = (bf16[768,2304]{1,0:T(8,128)(2,1)S(1)}, bf16[768,2304]{1,0:T(8,128)(2,1)}, u32[]{:S(2)}) copy-start(bf16[768,2304]{1,0:T(8,128)(2,1)} %param.25) | copy-start | bytes 10616836
  7.2 177.7 %all-gather.3.cloned.1.call-start = ((), (), s32[]{:S(2)}) async-start(), calls=%async_computation | async-start | bytes 1474560 | tf_op jit(solution)/shard_map/all_gather | solution.py:80
  7.9 190.1 %all-gather.5.cloned.1.call-start = ((), (), s32[]{:S(2)}) async-start(), calls=%async_computation.1 | async-start | bytes 1474560 | tf_op jit(solution)/shard_map/all_gather | solution.py:81
  8.7 590.5 %all-reduce.4.cloned.1.call-start = ((), (), s32[]{:S(2)}) async-start(), calls=%async_computation.2 | async-start | bytes 14155776 | tf_op jit(solution)/shard_map/psum | solution.py:273
  38.9 8.2 %copy-start.27 = (s32[1,1024]{1,0:T(1,128)S(1)}, s32[1,1024]{1,0:T(1,128)}, u32[]{:S(2)}) copy-start(s32[1,1024]{1,0:T(1,128)} %param.23) | copy-start | bytes 12292
  49.0 26.7 %copy-start.3 = (bf16[1024,12,64]{0,2,1:T(8,128)(2,1)S(1)}, bf16[1024,12,64]{0,2,1:T(8,128)(2,1)}, u32[]{:S(2)}) copy-start(bf16[1024,12,64]{0,2,1:T(8,128)(2,1)} %get-tuple-element.502) | copy-start | bytes 4718596 | tf_op jit(solution)/shard_map/while/body/eval_jaxpr/while
  63.4 15.4 %copy-start.1 = (f32[12,512,1024]{2,1,0:T(8,128)S(1)}, f32[12,512,1024]{2,1,0:T(8,128)}, u32[]{:S(2)}) copy-start(f32[12,512,1024]{2,1,0:T(8,128)} %get-tuple-element.454) | copy-start | bytes 75497472 | tf_op jit(solution)/shard_map/while/body/eval_jaxpr/while
  78.8 8.5 %copy-start.38 = (f32[2,12,512]{2,1,0:T(8,128)S(1)}, f32[2,12,512]{2,1,0:T(8,128)}, u32[]{:S(2)}) copy-start(f32[2,12,512]{2,1,0:T(8,128)} %get-tuple-element.485) | copy-start | bytes 147460 | tf_op jit(solution)/shard_map/while/body/eval_jaxpr/while
  89.6 26.7 %copy-start.3 = (bf16[1024,12,64]{0,2,1:T(8,128)(2,1)S(1)}, bf16[1024,12,64]{0,2,1:T(8,128)(2,1)}, u32[]{:S(2)}) copy-start(bf16[1024,12,64]{0,2,1:T(8,128)(2,1)} %get-tuple-element.502) | copy-start | bytes 4718596 | tf_op jit(solution)/shard_map/while/body/eval_jaxpr/while
  104.0 15.4 %copy-start.1 = (f32[12,512,1024]{2,1,0:T(8,128)S(1)}, f32[12,512,1024]{2,1,0:T(8,128)}, u32[]{:S(2)}) copy-start(f32[12,512,1024]{2,1,0:T(8,128)} %get-tuple-element.454) | copy-start | bytes 75497472 | tf_op jit(solution)/shard_map/while/body/eval_jaxpr/while
  119.4 8.5 %copy-start.38 = (f32[2,12,512]{2,1,0:T(8,128)S(1)}, f32[2,12,512]{2,1,0:T(8,128)}, u32[]{:S(2)}) copy-start(f32[2,12,512]{2,1,0:T(8,128)} %get-tuple-element.485) | copy-start | bytes 147460 | tf_op jit(solution)/shard_map/while/body/eval_jaxpr/while
  130.0 3.6 copy-start.20
  130.0 3.6 copy-start.55
  135.2 9.5 %copy-start.9 = (f32[1024,768]{0,1:T(8,128)}, f32[1024,768]{0,1:T(8,128)S(1)}, u32[]{:S(2)}) copy-start(f32[1024,768]{0,1:T(8,128)S(1)} %get-tuple-element.323) | copy-start | bytes 9437188
  135.3 136.0 %copy-start.29 = (f32[1024]{0:T(1024)}, f32[1024]{0:T(1024)S(1)}, u32[]{:S(2)}) copy-start(f32[1024]{0:T(1024)S(1)} %broadcast_multiply_fusion.5) | copy-start | bytes 12292
  135.3 9.5 %slice-start.5 = ((s8[4718592]{0:T(1024)(128)(4,1)}), s8[4194304]{0:T(1024)(128)(4,1)S(1)}, s32[]{:S(2)}) async-start(s8[4718592]{0:T(1024)(128)(4,1)} %bitcast.167), calls=%async_computation.8 | async-start | bytes 8388608
  136.2 135.0 %copy-start.31 = (f32[1024]{0:T(1024)}, f32[1024]{0:T(1024)S(1)}, u32[]{:S(2)}) copy-start(f32[1024]{0:T(1024)S(1)} %add_rsqrt_fusion.1) | copy-start | bytes 12292
  136.2 8.6 %slice-start.6 = ((s8[4718592]{0:T(1024)(128)(4,1)}), s8[524288]{0:T(1024)(128)(4,1)S(1)}, s32[]{:S(2)}) async-start(s8[4718592]{0:T(1024)(128)(4,1)} %bitcast.167), calls=%async_computation.9 | async-start | bytes 1048576
  136.2 8.6 %copy-start.56 = (f32[3072]{0:T(1024)S(1)}, f32[3072]{0:T(1024)}, u32[]{:S(2)}) copy-start(f32[3072]{0:T(1024)} %param.28) | copy-start | bytes 36868
  179.6 86.0 %copy-start.36 = (f32[1024]{0:T(1024)}, f32[1024]{0:T(1024)S(1)}, u32[]{:S(2)}) copy-start(f32[1024]{0:T(1024)S(1)} %broadcast_multiply_fusion.4) | copy-start | bytes 12292
  205.2 6.6 %copy-start.6 = (f32[1024,768]{0,1:T(8,128)S(1)}, f32[1024,768]{0,1:T(8,128)}, u32[]{:S(2)}) copy-start(f32[1024,768]{0,1:T(8,128)} %get-tuple-element.326) | copy-start | bytes 9437188
  205.2 6.6 %copy-start.16 = (bf16[16,48,768]{2,0,1:T(8,128)(2,1)S(1)}, bf16[16,48,768]{2,0,1:T(8,128)(2,1)}, u32[]{:S(2)}) copy-start(bf16[16,48,768]{2,0,1:T(8,128)(2,1)} %all-gather.5.cloned.1.call-done) | copy-start | bytes 3538948
  211.9 4.5 copy-start.60
  226.7 5.2 copy-start.5
  226.7 5.2 copy-start.12
  226.7 5.2 copy-start.14
  226.8 5.2 copy-start.24
  226.8 5.2 copy-start.41
  226.8 5.2 copy-start.44
  226.8 9.6 %slice-start = ((s8[12582912]{0:T(1024)(128)(4,1)}), s8[4194304]{0:T(1024)(128)(4,1)S(1)}, s32[]{:S(2)}) async-start(s8[12582912]{0:T(1024)(128)(4,1)} %bitcast.149), calls=%async_computation.3 | async-start | bytes 8388608
  226.8 9.6 %slice-start.1 = ((s8[12582912]{0:T(1024)(128)(4,1)}), s8[4194304]{0:T(1024)(128)(4,1)S(1)}, s32[]{:S(2)}) async-start(s8[12582912]{0:T(1024)(128)(4,1)} %bitcast.149), calls=%async_computation.4 | async-start | bytes 8388608
  232.0 4.4 slice-start.2
  232.0 4.4 copy-start.57
  236.4 15.1 %copy-start.10 = (f32[1024,768]{0,1:T(8,128)S(1)}, f32[1024,768]{0,1:T(8,128)}, u32[]{:S(2)}) copy-start(f32[1024,768]{0,1:T(8,128)} %copy-done.9) | copy-start | bytes 9437188
  251.5 14.0 %copy-start.51 = (f32[768]{0:T(1024)S(1)}, f32[768]{0:T(1024)}, u32[]{:S(2)}) copy-start(f32[768]{0:T(1024)} %param.33) | copy-start | bytes 9220
  271.3 7.8 %copy-start.28 = (s32[1,1024]{1,0:T(1,128)S(1)}, s32[1,1024]{1,0:T(1,128)}, u32[]{:S(2)}) copy-start(s32[1,1024]{1,0:T(1,128)} %param.23) | copy-start | bytes 12292
  279.1 243.6 %copy-start.37 = (f32[1024]{0:T(1024)S(1)}, f32[1024]{0:T(1024)}, u32[]{:S(2)}) copy-start(f32[1024]{0:T(1024)} %copy-done.36) | copy-start | bytes 12292
  279.1 243.6 %copy-start.42 = (f32[1024]{0:T(1024)S(1)}, f32[1024]{0:T(1024)}, u32[]{:S(2)}) copy-start(f32[1024]{0:T(1024)} %copy-done.40) | copy-start | bytes 12292
  279.1 243.6 %copy-start.45 = (f32[768]{0:T(1024)S(1)}, f32[768]{0:T(1024)}, u32[]{:S(2)}) copy-start(f32[768]{0:T(1024)} %param.32) | copy-start | bytes 9220
  283.0 14.6 %copy-start.8 = (f32[12,512]{1,0:T(8,128)}, f32[12,512]{1,0:T(8,128)S(1)}, u32[]{:S(2)}) copy-start(f32[12,512]{1,0:T(8,128)S(1)} %constant_dynamic-slice_fusion.2) | copy-start | bytes 73732 | tf_op jit(solution)/shard_map/while/body/eval_jaxpr/while
  283.4 14.3 %copy-start.2 = (pred[512,1024]{1,0:T(8,128)(4,1)}, pred[512,1024]{1,0:T(8,128)(4,1)S(1)}, u32[]{:S(2)}) copy-start(pred[512,1024]{1,0:T(8,128)(4,1)S(1)} %broadcast_compare_fusion.5) | copy-start | bytes 1572868 | tf_op jit(solution)/shard_map/while/body/eval_jaxpr/while
  283.4 14.3 %copy-start.13 = (bf16[1024,12,64]{0,2,1:T(8,128)(2,1)S(1)}, bf16[1024,12,64]{0,2,1:T(8,128)(2,1)}, u32[]{:S(2)}) copy-start(bf16[1024,12,64]{0,2,1:T(8,128)(2,1)} %get-tuple-element.551) | copy-start | bytes 4718596 | tf_op jit(solution)/shard_map/while/body/eval_jaxpr/while
  403.7 14.7 %copy-start.8 = (f32[12,512]{1,0:T(8,128)}, f32[12,512]{1,0:T(8,128)S(1)}, u32[]{:S(2)}) copy-start(f32[12,512]{1,0:T(8,128)S(1)} %constant_dynamic-slice_fusion.2) | copy-start | bytes 73732 | tf_op jit(solution)/shard_map/while/body/eval_jaxpr/while
  404.1 14.4 %copy-start.2 = (pred[512,1024]{1,0:T(8,128)(4,1)}, pred[512,1024]{1,0:T(8,128)(4,1)S(1)}, u32[]{:S(2)}) copy-start(pred[512,1024]{1,0:T(8,128)(4,1)S(1)} %broadcast_compare_fusion.5) | copy-start | bytes 1572868 | tf_op jit(solution)/shard_map/while/body/eval_jaxpr/while
  404.1 14.4 %copy-start.13 = (bf16[1024,12,64]{0,2,1:T(8,128)(2,1)S(1)}, bf16[1024,12,64]{0,2,1:T(8,128)(2,1)}, u32[]{:S(2)}) copy-start(bf16[1024,12,64]{0,2,1:T(8,128)(2,1)} %get-tuple-element.551) | copy-start | bytes 4718596 | tf_op jit(solution)/shard_map/while/body/eval_jaxpr/while
  551.7 3.2 copy-start.46
  551.7 3.2 copy-start.47
  599.1 3.4 copy-start.18
  (31 other events, 56.5 us)
Sparse Core Ops, SparseCore 0:
  9.6 20.1 all-gather.2
  31.3 17.4 all-gather.4
  271.4 167.5 all-reduce.3
where the time goes:
time: 625 us; the launch traced here: 614 us
  matrix products  435 us (70%)
  local copies, waits for them, and re-layouts  67.6 us (11%)
  other arithmetic  46 us (7%)
  blocking collectives  42.9 us (7%)
  between operations  17.1 us (3%)
    dot_general x2, matrix products, block_step(): jnp.einsum('hqk,khd->qhd', grad_logits, keys_wide, precision=lax.Precisio...  81.4 us
    dot_general x9, matrix products, matmul(): return jnp.dot(left_op, right_op, preferred_element_type=jnp.float32)  74 us
    dot_general x8, matrix products, contract_cols(): lax.dot_general(left_op, right_op, (((1,), (1,)), ((), ())), preferred_el...  61.3 us
    dot_general x2, matrix products, block_step(): jnp.einsum('hqk,qhd->khd', grad_logits, queries_blk_wide, precision=lax.P...  59.6 us
    dot_general x4, matrix products, block_logits(): jnp.einsum('qhd,khd->hqk', queries_blk, key_heads, preferred_element_type...  57.3 us
    psum x1, blocking collectives, per_device(): lax.psum((query_grad, key_grad, value_grad, bias_grad, gain_one_grad, shi...  42.9 us
    dot_general x2, matrix products, block_step(): jnp.einsum('qhd,khd->hqk', grad_blk, value_heads, preferred_element_type=...  37.9 us
    dot_general x2, matrix products, block_step(): jnp.einsum('hqk,qhd->khd', prob_low, grad_blk, preferred_element_type=jnp...  28.2 us
  transfers between devices with their start and end apart: 3, of which 0 were waited for; matrix products, arithmetic and copies ran while one was open for 74% of the time, Pallas kernels for 0%

commit v1 on v0

v1 whole, which is shorter than its diff:
```python
import math

import jax
import jax.numpy as jnp
import functools

from jax import lax
from jax.experimental import pallas as pl
from jax.experimental.pallas import tpu as pltpu
from jax.sharding import PartitionSpec as P

D = 768
HEADS = 12
HEAD_DIM = 64
ADAPTERS = 16
BOTTLE = 48

AUG = 16
BF = jnp.bfloat16
F32 = jnp.float32
BLOCK_Q = 256
BLOCK_K = 128


def dot_on(left_op, right_op, left_dim, right_dim):
    return lax.dot_general(
        left_op,
        right_op,
        (((left_dim,), (right_dim,)), ((), ())),
        preferred_element_type=F32,
    )


def head_rows(part, head):
    return pl.ds(pl.multiple_of(part * D + head * HEAD_DIM, HEAD_DIM), HEAD_DIM)


def attend_kernel(bounds, x, w, seg, packed, ctx, lse, xt, qa, kt, m_s, l_s, o_s):
    seq = x.shape[0]
    xt[...] = x[...].T

    def project(step, unused):
        rows = pl.ds(pl.multiple_of(step * 256, 256), 256)
        packed[rows, :] = dot_on(w[:, rows], xt[...], 0, 0).astype(BF)
        return 0

    lax.fori_loop(0, w.shape[1] // 256, project, 0)
    row = lax.broadcasted_iota(jnp.int32, (AUG, seq), 0)
    same = row == seg[...]
    aug_q = jnp.where(same, 1.0, 0.0).astype(BF)
    aug_k = jnp.where((row < 4) & (~same), -1e30, 0.0).astype(BF)

    def prepare(head, unused):
        qa[head, :HEAD_DIM, :] = packed[head_rows(0, head), :] * jnp.asarray(0.125, BF)
        qa[head, HEAD_DIM:, :] = aug_q
        kt[head] = jnp.concatenate([packed[head_rows(1, head), :], aug_k], axis=0).T
        return 0

    lax.fori_loop(0, HEADS, prepare, 0)

    def query_block(i, unused):
        qs = pl.ds(pl.multiple_of(i * BLOCK_Q, BLOCK_Q), BLOCK_Q)
        for h in range(HEADS):
            m_s[h] = jnp.full((8, BLOCK_Q), -1e30, F32)
            l_s[h] = jnp.zeros((8, BLOCK_Q), F32)
            o_s[h] = jnp.zeros((HEAD_DIM, BLOCK_Q), F32)

        def key_block(j, unused):
            ks = pl.ds(pl.multiple_of(j * BLOCK_K, BLOCK_K), BLOCK_K)
            logits = [dot_on(kt[h, ks, :], qa[h, :, qs], 1, 0) for h in range(HEADS)]
            probs = []
            for h in range(HEADS):
                tile = logits[h].reshape(BLOCK_K // 8, 8, BLOCK_Q)
                top = jnp.max(jnp.max(tile, axis=0), axis=0, keepdims=True)
                old = m_s[h]
                new = jnp.maximum(old, jnp.broadcast_to(top, (8, BLOCK_Q)))
                decay = jnp.exp(old - new)
                prob = jnp.exp(tile - new[None])
                l_s[h] = l_s[h] * decay + jnp.sum(prob, axis=0)
                m_s[h] = new
                probs.append((prob.reshape(BLOCK_K, BLOCK_Q).astype(BF), decay))
            for h in range(HEADS):
                prob, decay = probs[h]
                part = dot_on(packed[2 * D + h * HEAD_DIM : 2 * D + (h + 1) * HEAD_DIM, ks], prob, 1, 0)
                kept = o_s[h].reshape(8, 8, BLOCK_Q) * decay[None]
                o_s[h] = kept.reshape(HEAD_DIM, BLOCK_Q) + part
            return 0

        lax.fori_loop(bounds[0, i], bounds[1, i], key_block, 0)
        for h in range(HEADS):
            total = jnp.sum(l_s[h], axis=0, keepdims=True)
            ctx[h * HEAD_DIM : (h + 1) * HEAD_DIM, qs] = (o_s[h] * (1.0 / total)).astype(BF)
            lse[h, :, qs] = m_s[h][:1] + jnp.log(total)
        return 0

    lax.fori_loop(0, seq // BLOCK_Q, query_block, 0)


def attend_back_kernel(bounds, packed, ctx, lse, gctx, seg, gp, qa, kt, da, vt, dq_s, dk_s, dv_s):
    seq = packed.shape[1]
    row = lax.broadcasted_iota(jnp.int32, (AUG, seq), 0)
    same = row == seg[...]
    aug_q = jnp.where(same, 1.0, 0.0)
    aug_k = jnp.where(row < 4, jnp.where(same, 0.0, -1e30), jnp.where(row < 7, 1.0, 0.0)).astype(BF)
    aug_v = jnp.where(row < 3, 1.0, 0.0).astype(BF)

    def minus_rows(value, base):
        rest = -value
        rows = jnp.zeros((AUG, seq), F32)
        for step in range(3):
            piece = rest.astype(BF).astype(F32)
            rows = jnp.where(row == base + step, jnp.broadcast_to(piece, (AUG, seq)), rows)
            rest = rest - piece
        return rows

    def prepare(head, unused):
        rows = head_rows(0, head)
        qa[head, :HEAD_DIM, :] = packed[rows, :] * jnp.asarray(0.125, BF)
        qa[head, HEAD_DIM:, :] = (aug_q + minus_rows(lse[head], 4)).astype(BF)
        kt[head] = jnp.concatenate([packed[head_rows(1, head), :], aug_k], axis=0).T
        vt[head] = jnp.concatenate([packed[head_rows(2, head), :], aug_v], axis=0).T
        grad = gctx[rows, :]
        inner = jnp.sum(grad.astype(F32) * ctx[rows, :].astype(F32), axis=0, keepdims=True)
        da[head, :HEAD_DIM, :] = grad
        da[head, HEAD_DIM:, :] = minus_rows(inner, 0).astype(BF)
        dk_s[head] = jnp.zeros((HEAD_DIM, seq), F32)
        dv_s[head] = jnp.zeros((HEAD_DIM, seq), F32)
        return 0

    lax.fori_loop(0, HEADS, prepare, 0)

    def query_block(i, unused):
        qs = pl.ds(pl.multiple_of(i * BLOCK_Q, BLOCK_Q), BLOCK_Q)
        for h in range(HEADS):
            dq_s[h] = jnp.zeros((HEAD_DIM, BLOCK_Q), F32)

        def key_block(j, unused):
            ks = pl.ds(pl.multiple_of(j * BLOCK_K, BLOCK_K), BLOCK_K)
            first, second = {}, {}
            lag = 4
            for t in range(HEADS + 2 * lag):
                if t < HEADS:
                    first[t] = (
                        dot_on(kt[t, ks, :], qa[t, :, qs], 1, 0),
                        dot_on(vt[t, ks, :], da[t, :, qs], 1, 0),
                    )
                h = t - lag
                if 0 <= h < HEADS:
                    logits, grad = first.pop(h)
                    prob = jnp.exp(logits)
                    second[h] = (prob.astype(BF), (prob * grad).astype(BF))
                h = t - 2 * lag
                if 0 <= h < HEADS:
                    prob, grad = second.pop(h)
                    dv_s[h, :, ks] += dot_on(da[h, :HEAD_DIM, qs], prob, 1, 1)
                    dk_s[h, :, ks] += dot_on(qa[h, :HEAD_DIM, qs], grad, 1, 1)
                    dq_s[h] += dot_on(packed[D + h * HEAD_DIM : D + (h + 1) * HEAD_DIM, ks], grad, 1, 0)
            return 0

        lax.fori_loop(bounds[0, i], bounds[1, i], key_block, 0)
        for h in range(HEADS):
            gp[h * HEAD_DIM : (h + 1) * HEAD_DIM, qs] = (dq_s[h] * 0.125).astype(BF)
        return 0

    lax.fori_loop(0, seq // BLOCK_Q, query_block, 0)

    def finish(head, unused):
        gp[head_rows(1, head), :] = dk_s[head].astype(BF)
        gp[head_rows(2, head), :] = dv_s[head].astype(BF)
        return 0

    lax.fori_loop(0, HEADS, finish, 0)


def key_bounds(seg):
    first = seg[::BLOCK_Q]
    last = seg[BLOCK_Q - 1 :: BLOCK_Q]
    low = jnp.sum((seg[None, :] < first[:, None]).astype(jnp.int32), axis=1)
    high = jnp.sum((seg[None, :] <= last[:, None]).astype(jnp.int32), axis=1)
    return jnp.stack([low // BLOCK_K, (high + BLOCK_K - 1) // BLOCK_K])


def in_vmem():
    return pl.BlockSpec(memory_space=pltpu.VMEM)


def attend(x, w, seg, bounds):
    seq = x.shape[0]
    return pl.pallas_call(
        attend_kernel,
        in_specs=[pl.BlockSpec(memory_space=pltpu.SMEM), in_vmem(), in_vmem(), in_vmem()],
        out_specs=[in_vmem(), in_vmem(), in_vmem()],
        out_shape=(
            jax.ShapeDtypeStruct((3 * D, seq), BF),
            jax.ShapeDtypeStruct((D, seq), BF),
            jax.ShapeDtypeStruct((HEADS, 1, seq), F32),
        ),
        scratch_shapes=[
            pltpu.VMEM((D, seq), BF),
            pltpu.VMEM((HEADS, HEAD_DIM + AUG, seq), BF),
            pltpu.VMEM((HEADS, seq, HEAD_DIM + AUG), BF),
            pltpu.VMEM((HEADS, 8, BLOCK_Q), F32),
            pltpu.VMEM((HEADS, 8, BLOCK_Q), F32),
            pltpu.VMEM((HEADS, HEAD_DIM, BLOCK_Q), F32),
        ],
        name="attend",
        compiler_params=pltpu.CompilerParams(vmem_limit_bytes=60 << 20),
    )(bounds, x, w, seg)


def attend_back(packed, ctx, lse, gctx, seg, bounds):
    seq = packed.shape[1]
    aug = HEAD_DIM + AUG
    return pl.pallas_call(
        attend_back_kernel,
        in_specs=[pl.BlockSpec(memory_space=pltpu.SMEM)] + [in_vmem() for _ in range(5)],
        out_specs=in_vmem(),
        out_shape=jax.ShapeDtypeStruct((3 * D, seq), BF),
        scratch_shapes=[
            pltpu.VMEM((HEADS, aug, seq), BF),
            pltpu.VMEM((HEADS, seq, aug), BF),
            pltpu.VMEM((HEADS, aug, seq), BF),
            pltpu.VMEM((HEADS, seq, aug), BF),
            pltpu.VMEM((HEADS, HEAD_DIM, BLOCK_Q), F32),
            pltpu.VMEM((HEADS, HEAD_DIM, seq), F32),
            pltpu.VMEM((HEADS, HEAD_DIM, seq), F32),
        ],
        name="attend_back",
        compiler_params=pltpu.CompilerParams(vmem_limit_bytes=62 << 20),
    )(bounds, packed, ctx, lse, gctx, seg)


def matmul(left_op, right_op):
    return jnp.dot(left_op, right_op, preferred_element_type=jnp.float32)


def contract_rows(left_op, right_op):
    return lax.dot_general(
        left_op, right_op, (((0,), (0,)), ((), ())), preferred_element_type=jnp.float32
    )


def contract_cols(left_op, right_op):
    return lax.dot_general(
        left_op, right_op, (((1,), (1,)), ((), ())), preferred_element_type=jnp.float32
    )


def normalize(values):
    centre = values - jnp.mean(values, axis=-1, keepdims=True)
    factor = lax.rsqrt(jnp.mean(centre * centre, axis=-1, keepdims=True) + 1e-06)
    return (centre * factor, factor)


def norm_back(grad_out, unit_vals, factor, gain_vec):
    scaled = grad_out * gain_vec
    return factor * (
        scaled
        - jnp.mean(scaled, axis=-1, keepdims=True)
        - unit_vals * jnp.mean(scaled * unit_vals, axis=-1, keepdims=True)
    )


def gelu_slope(values):
    return 0.5 * (1.0 + lax.erf(values * (1.0 / math.sqrt(2.0)))) + values * jnp.exp(
        -0.5 * values * values
    ) * (1.0 / math.sqrt(2.0 * math.pi))


def per_device(
    block_input,
    segments,
    real_mask,
    qkv_weight,
    attn_out_weight,
    ffn_in_weight,
    ffn_bias,
    ffn_out_weight,
    first_gain,
    first_shift,
    second_gain,
    second_shift,
    adapter_down,
    adapter_up,
    joining_query,
    joining_key,
    joining_value,
    cotangent,
):
    row_count, seq_len, width = block_input.shape
    token_count = row_count * seq_len
    mix_scale = 1.0 / math.sqrt(D)
    bank_width = ADAPTERS * BOTTLE
    down_full, up_full = (
        lax.all_gather(adapter_down, "narrow", axis=2, tiled=True),
        lax.all_gather(adapter_up, "narrow", axis=1, tiled=True),
    )
    down_flat = down_full.reshape(width, bank_width)
    up_flat = up_full.reshape(bank_width, width)

    tokens = block_input.reshape(token_count, width)
    seg_row = segments.reshape(1, token_count)
    bounds = key_bounds(segments.reshape(token_count))
    packed, context, log_total = attend(tokens, qkv_weight, seg_row, bounds)
    attn_out = contract_rows(context, attn_out_weight)
    unit_one, factor_one = normalize(tokens.astype(jnp.float32) + attn_out)
    h_one = unit_one * first_gain + first_shift
    ffn_pre = matmul(h_one.astype(jnp.bfloat16), ffn_in_weight) + ffn_bias
    act_low = jax.nn.gelu(ffn_pre, approximate=False).astype(jnp.bfloat16)
    ffn_out = matmul(act_low, ffn_out_weight)
    unit_two, factor_two = normalize(h_one + ffn_out)
    h_two = unit_two * second_gain + second_shift
    h_low = h_two.astype(jnp.bfloat16)
    query_low = matmul(h_low, joining_query).astype(jnp.bfloat16)
    probe_low = contract_cols(query_low, joining_key).astype(jnp.bfloat16)
    down_pre = matmul(h_low, down_flat)
    bottle = jax.nn.gelu(down_pre, approximate=False).reshape(token_count, ADAPTERS, BOTTLE)
    guide = contract_cols(probe_low, up_flat).reshape(token_count, ADAPTERS, BOTTLE)
    scores = jnp.sum(bottle * guide, axis=-1) * mix_scale
    shifted = scores - jnp.max(scores, axis=-1, keepdims=True)
    log_weights = shifted - jnp.log(jnp.sum(jnp.exp(shifted), axis=-1, keepdims=True))
    mix_weights = jnp.exp(log_weights)
    mixed_low = (
        (mix_weights[:, :, None] * bottle).reshape(token_count, bank_width).astype(jnp.bfloat16)
    )
    update = matmul(mixed_low, up_flat)
    blend_low = (h_two + update).astype(jnp.bfloat16)
    block_output = (h_two + matmul(blend_low, joining_value)).astype(jnp.bfloat16)
    real_rows = real_mask.reshape(token_count).astype(jnp.float32)
    ent_local = jnp.sum(-jnp.sum(mix_weights * log_weights, axis=-1) * real_rows)
    count_local = jnp.sum(real_rows)
    ent_total = lax.psum(ent_local, ("wide", "narrow"))
    grad_out = cotangent.reshape(token_count, width)
    value_grad = contract_rows(blend_low, grad_out)
    grad_blend = contract_cols(grad_out, joining_value)
    grad_update = grad_blend.astype(jnp.bfloat16)
    grad_mixed = contract_cols(grad_update, up_flat).reshape(token_count, ADAPTERS, BOTTLE)
    grad_weights = jnp.sum(grad_mixed * bottle, axis=-1)
    grad_scores = mix_weights * (
        grad_weights - jnp.sum(grad_weights * mix_weights, axis=-1, keepdims=True)
    )
    score_term = (grad_scores * mix_scale)[:, :, None]
    grad_guide = (score_term * bottle).reshape(token_count, bank_width)
    grad_bottle = (grad_mixed * mix_weights[:, :, None] + score_term * guide).reshape(
        token_count, bank_width
    )
    grad_down = grad_bottle * gelu_slope(down_pre)
    grad_probe = matmul(grad_guide.astype(BF), up_flat).astype(BF)
    key_grad = contract_rows(grad_probe, query_low)
    grad_query = matmul(grad_probe, joining_key).astype(jnp.bfloat16)
    query_grad = contract_rows(h_low, grad_query)
    adapter_back = contract_cols(grad_down.astype(BF), down_flat)
    grad_h_two = (
        grad_out.astype(jnp.float32)
        + grad_blend
        + adapter_back
        + contract_cols(grad_query, joining_query)
    )
    gain_two_grad = jnp.sum(grad_h_two * unit_two, axis=0)
    shift_two_grad = jnp.sum(grad_h_two, axis=0)
    grad_r_two = norm_back(grad_h_two, unit_two, factor_two, second_gain)
    grad_ffn = grad_r_two.astype(jnp.bfloat16)
    grad_pre = (contract_cols(grad_ffn, ffn_out_weight) * gelu_slope(ffn_pre)).astype(jnp.bfloat16)
    bias_grad = jnp.sum(grad_pre.astype(jnp.float32), axis=0)
    grad_h_one = grad_r_two + contract_cols(grad_pre, ffn_in_weight)
    gain_one_grad = jnp.sum(grad_h_one * unit_one, axis=0)
    shift_one_grad = jnp.sum(grad_h_one, axis=0)
    grad_r_one = norm_back(grad_h_one, unit_one, factor_one, first_gain)
    grad_attn = grad_r_one.astype(jnp.bfloat16)
    grad_context = contract_cols(attn_out_weight, grad_attn).astype(BF)
    grad_packed = attend_back(packed, context, log_total, grad_context, seg_row, bounds)
    input_grad = (grad_r_one + lax.dot_general(grad_packed, qkv_weight, (((0,), (1,)), ((), ())), preferred_element_type=F32)).astype(jnp.bfloat16)
    summed_all = lax.psum(
        (
            query_grad,
            key_grad,
            value_grad,
            bias_grad,
            gain_one_grad,
            shift_one_grad,
            gain_two_grad,
            shift_two_grad,
            count_local,
        ),
        ("wide", "narrow"),
    )
    summed = summed_all[:8]
    count_total = summed_all[8]
    entropy = ent_total / count_total
    return (
        block_output.reshape(row_count, seq_len, width),
        input_grad.reshape(row_count, seq_len, width),
        summed[0],
        summed[1],
        summed[2],
        summed[3],
        summed[4],
        summed[5],
        summed[6],
        summed[7],
        entropy,
    )


def solution(mesh):
    placed = (
        P(("wide", "narrow"), None, None),
        P(("wide", "narrow"), None),
        P(("wide", "narrow"), None),
        P(),
        P(),
        P(),
        P(),
        P(),
        P(),
        P(),
        P(),
        P(),
        P(None, None, "narrow"),
        P(None, "narrow", None),
        P(),
        P(),
        P(),
        P(("wide", "narrow"), None, None),
    )
    return jax.shard_map(
        per_device,
        mesh=mesh,
        in_specs=placed,
        out_specs=(
            P(("wide", "narrow"), None, None),
            P(("wide", "narrow"), None, None),
            P(),
            P(),
            P(),
            P(),
            P(),
            P(),
            P(),
            P(),
            P(),
        ),
        check_vma=False,
    )
```

time: 625 us -> 359 us (0.57)
  matrix products: 435 us -> 145 us
  Pallas kernels: 0 us -> 61.7 us
  waiting for transfers between devices: 1.42 us -> 58.6 us
  local copies, waits for them, and re-layouts: 67.6 us -> 16.6 us
  other arithmetic: 46 us -> 9.65 us
    dot_general x16 -> x1, matrix products: 291 us -> 7.29 us  [per_device(): lax.dot_general(grad_packed, qkv_weight, (((0,), (1,)), ((), ())), prefer...]
    pallas_call x0 -> x2, Pallas kernels: none -> 61.7 us  [the longest x1 32.2 us: attend_back(): pl.pallas_call(attend_back_kernel, in_specs=[pl.BlockSpec(memory_space=pl...]
    psum x1, waiting for transfers between devices: 0.02 us -> 57.2 us  [per_device(): lax.psum((query_grad, key_grad, value_grad, bias_grad, gain_one_grad, shi...]
    reduce_sum x2 -> x1, other arithmetic: 24.6 us -> 0.9 us  [key_bounds(): low = jnp.sum((seg[None, :] < first[:, None]).astype(jnp.int32), axis=1)]
    while x30 -> x0, local copies, waits for them, and re-layouts: 14.8 us -> none
    unnamed x134 -> x77, local copies, waits for them, and re-layouts: 27.2 us -> 13.1 us
    convert_element_type x1 -> x0, local copies, waits for them, and re-layouts: 6.65 us -> none  [per_device(): packed = matmul(tokens, qkv_weight).astype(jnp.bfloat16)]
    dot_general x9 -> x8, matrix products: 74 us -> 70.5 us  [matmul(): return jnp.dot(left_op, right_op, preferred_element_type=jnp.float32)]
  transfers between devices with their start and end apart: 3 -> 3, of which waited for: 0 -> 1; matrix products, arithmetic and copies ran while one was open for 74% -> 31% of each run, Pallas kernels for 0% -> 17%
where the time goes in v1:
time: 359 us; the launch traced here: 353 us
  matrix products  145 us (40%)
  Pallas kernels  61.7 us (17%)
  waiting for transfers between devices  58.6 us (16%)
  blocking collectives  44.1 us (12%)
  between operations  17.2 us (5%)
  local copies, waits for them, and re-layouts  16.6 us (5%)
  other arithmetic  9.65 us (3%)
    dot_general x8, matrix products, matmul(): return jnp.dot(left_op, right_op, preferred_element_type=jnp.float32)  70.5 us
    psum x1, waiting for transfers between devices, per_device(): lax.psum((query_grad, key_grad, value_grad, bias_grad, gain_one_grad, shi...  57.2 us
    dot_general x8, matrix products, contract_cols(): lax.dot_general(left_op, right_op, (((1,), (1,)), ((), ())), preferred_el...  55.3 us
    psum x1, blocking collectives, per_device(): lax.psum((query_grad, key_grad, value_grad, bias_grad, gain_one_grad, shi...  44.1 us
    pallas_call x1, Pallas kernels, attend_back(): pl.pallas_call(attend_back_kernel, in_specs=[pl.BlockSpec(memory_space=pl...  32.2 us
    pallas_call x1, Pallas kernels, attend(): pl.pallas_call(attend_kernel, in_specs=[pl.BlockSpec(memory_space=pltpu.S...  29.5 us
    unnamed x77, local copies, waits for them, and re-layouts  13.1 us
    dot_general x4, matrix products, contract_rows(): lax.dot_general(left_op, right_op, (((0,), (0,)), ((), ())), preferred_el...  12.1 us
  transfers between devices with their start and end apart: 3, of which 1 were waited for; matrix products, arithmetic and copies ran while one was open for 31% of the time, Pallas kernels for 17%

profile of v1, /device:TPU:0, one launch (start us, length us, event | category | flops | bytes accessed | tf_op | source)
XLA Modules:
  0.0 353.1 jit_solution(14632168394986662913)
XLA Ops:
  7.2 0.7 all-gather.3.cloned.1.call-update
  8.0 0.7 all-gather.5.cloned.1.call-update
  8.7 0.8 slice.6
  9.5 0.8 slice.7
  10.3 1.3 convert_element_type.101
  11.6 1.3 convert_reduce_fusion.3
  12.9 0.9 convert_reduce_fusion.2
  13.8 0.6 pad_add_fusion.bounds
  14.4 29.5 %attend.1 = (bf16[2304,1024]{1,0:T(8,128)(2,1)}, bf16[768,1024]{1,0:T(8,128)(2,1)}, f32[12,1,1024]{2,1,0:T(1,128)}) custom-call(s32[2,4]{1,0:T(2,128)} %pad_add_fusion.bounds, bf16[1024,768]{1,0:T(8,128)(2,1)} %bitcast.88, bf16[768,2304]{1,0:T(8,128)(2,1)} %w.1, s32[1,1024]{1,0:T(1,128)} %seg.3), custom_call_target="tpu_custom_call" | custom-call | tf_op jit(solution)/shard_map/attend/pallas_call | solution.py:189
  43.9 3.5 fusion.94
  48.2 5.2 %fusion.40 = f32[1024,3072]{1,0:T(8,128)S(1)} fusion(bf16[768,3072]{1,0:T(8,128)(2,1)S(1)} %bitcast.100, f32[1024,768]{1,0:T(8,128)S(1)} %get-tuple-element.46, f32[768]{0:T(1024)S(1)} %copy-done.28, f32[768]{0:T(1024)S(1)} %copy-done.29, f32[1024]{0:T(1024)S(1)} %add_rsqrt_fusion.1, f32[1024]{0:T(1024)S(1)} %broadcast_multiply_fusion.5), kind=kOutput, calls=%fused_computation.88 | convolution fusion | flops 4835770368 | bytes 20461568 | tf_op jit(solution)/shard_map/dot_general | solution.py:234
  53.5 43.4 %fusion.95 = (f32[1024]{0:T(1024)S(1)}, f32[1024,768]{1,0:T(8,128)S(1)}) fusion(bf16[3072,768]{1,0:T(8,128)(2,1)S(1)} %bitcast.98, f32[1024,3072]{1,0:T(8,128)S(1)} %fusion.40, f32[3072]{0:T(1024)S(1)} %copy-done.27, f32[768]{0:T(1024)S(1)} %copy-done.28, f32[768]{0:T(1024)S(1)} %copy-done.29, f32[1024]{0:T(1024)S(1)} %add_rsqrt_fusion.1, ...), kind=kOutput, calls=%fused_computation.170 | convolution fusion | flops 5044173824 | bytes 23623680 | tf_op jit(solution)/shard_map/dot_general | solution.py:234
  97.8 0.5 fusion.37
  98.7 2.5 convolution_convert_fusion.4
  101.2 3.1 fusion.46
  104.3 1.6 copy.51
  105.9 1.0 copy-done.19
  106.9 9.2 %fusion.19 = (f32[1024,768]{0,1:T(8,128)}, f32[1024,768]{0,1:T(8,128)}) fusion(bf16[1024,768]{1,0:T(8,128)(2,1)S(1)} %fusion.37, bf16[768,768]{0,1:T(8,128)(2,1)S(1)} %bitcast.89), kind=kOutput, calls=%fused_computation.31 | convolution fusion | flops 1258291200 | bytes 9043968 | tf_op jit(solution)/shard_map/dot_general | solution.py:234
  116.1 7.2 %fusion.48 = f32[1024,16,48]{0,2,1:T(8,128)} fusion(bf16[1024,768]{1,0:T(8,128)(2,1)} %convolution_convert_fusion.4, bf16[768,768]{1,0:T(8,128)(2,1)} %param.33, bf16[16,48,768]{2,0,1:T(8,128)(2,1)} %all-gather.5.cloned.1.call-done), kind=kOutput, calls=%fused_computation.95 | convolution fusion | flops 2416705536 | bytes 7077888 | tf_op jit(solution)/shard_map/dot_general | solution.py:244
  123.3 5.6 %multiply_reduce_fusion.4 = (f32[1024,16]{0,1:T(8,128)S(1)}, f32[1024,16]{0,1:T(8,128)S(1)}, f32[1024,16,48]{0,2,1:T(8,128)S(1)}) fusion(f32[1024,16,48]{0,2,1:T(8,128)} %bitcast.87, f32[1024,16,48]{0,2,1:T(8,128)} %fusion.48, bf16[16,48,768]{2,0,1:T(8,128)(2,1)S(1)} %copy-done.6, f32[1024,768]{1,0:T(8,128)} %fusion.46), kind=kOutput, calls=%fused_computation.51 | convolution fusion | flops 1211858944 | bytes 13893632 | tf_op jit(solution)/shard_map/dot_general | solution.py:244
  129.1 0.6 fusion.26
  130.0 1.4 convolution_convert_fusion.2
  131.5 1.4 convolution_convert_fusion.1
  132.9 2.9 fusion.98
  135.8 1.1 multiply_add_fusion
  136.9 0.8 copy-done.11
  137.7 1.5 fusion.25
  139.3 1.4 fusion.96
  140.7 2.9 fusion.97
  143.6 0.9 copy-done.5
  144.5 3.9 %multiply_reduce_fusion = (f32[768]{0:T(1024)S(1)}, f32[1024]{0:T(1024)S(1)}, f32[1024]{0:T(1024)S(1)}, f32[768]{0:T(1024)S(1)}, f32[1024,768]{1,0:T(8,128)}) fusion(f32[1024]{0:T(1024)S(1)} %add_rsqrt_fusion, f32[1024,768]{1,0:T(8,128)S(1)} %copy-done.2, f32[1024]{0:T(1024)S(1)} %broadcast_multiply_fusion.4, f32[768]{0:T(1024)S(1)} %copy-done.21, ...), kind=kOutput, calls=%fused_computation.42 | convolution fusion | flops 1218179584 | bytes 16933888 | tf_op jit(solution)/shard_map/dot_general | solution.py:244
  148.4 1.8 add_convert_fusion.2
  150.2 1.1 copy-done.30
  151.3 2.9 fusion.44
  154.2 15.0 %convert_reduce_fusion = (f32[3072]{0:T(1024)S(1)}, bf16[1024,3072]{1,0:T(8,128)(2,1)}) fusion(f32[1024,3072]{1,0:T(8,128)} %copy-done.32, f32[3072]{0:T(1024)S(1)} %copy-done.27, bf16[3072,768]{1,0:T(8,128)(2,1)} %param.25, f32[1024]{0:T(1024)S(1)} %broadcast_multiply_fusion.2, f32[1024]{0:T(1024)S(1)} %broadcast_multiply_fusion.3, ...), kind=kOutput, calls=%fused_computation.11 | convolution fusion | flops 4879021056 | bytes 29928448 | tf_op jit(solution)/shard_map/dot_general | solution.py:244
  169.2 13.1 %multiply_reduce_fusion.1 = (f32[768]{0:T(1024)S(1)}, f32[1024]{0:T(1024)S(1)}, f32[1024]{0:T(1024)S(1)}, f32[768]{0:T(1024)S(1)}, f32[1024,768]{1,0:T(8,128)}) fusion(f32[1024,768]{1,0:T(8,128)} %copy-done.9, f32[1024]{0:T(1024)S(1)} %add_rsqrt_fusion.1, f32[1024]{0:T(1024)S(1)} %broadcast_multiply_fusion.5, f32[768]{0:T(1024)S(1)} %copy-done.29, ...), kind=kOutput, calls=%fused_computation.43 | convolution fusion | flops 4845203456 | bytes 23638016 | tf_op jit(solution)/shard_map/dot_general | solution.py:244
  182.4 0.6 multiply_reduce_fusion.13
  183.0 44.1 %all-reduce = (f32[3072]{0:T(1024)}, f32[768]{0:T(1024)}, f32[768]{0:T(1024)}, f32[768]{0:T(1024)}, f32[768]{0:T(1024)}, /*index=5*/f32[]{:T(128)}, f32[]{:T(128)}) all-reduce(f32[3072]{0:T(1024)S(1)} %get-tuple-element.54, f32[768]{0:T(1024)S(1)} %get-tuple-element.19, ...), channel_id=1, replica_groups=mesh['wide'=8,'narrow'=4] {'wide','narrow'}, use_global_device_ids=true, to_apply=%region_19.20 | all-reduce | flops 6146 | bytes 49168 | tf_op jit(solution)/shard_map/psum | solution.py:373
  228.4 6.0 %fusion.58.gctx = bf16[768,1024]{1,0:T(8,128)(2,1)} fusion(bf16[768,768]{1,0:T(8,128)(2,1)S(1)} %copy-done.25, f32[1024,768]{1,0:T(8,128)} %get-tuple-element.53, f32[1024,768]{1,0:T(8,128)} %copy-done.9, f32[1024]{0:T(1024)S(1)} %broadcast_multiply_fusion, f32[1024]{0:T(1024)S(1)} %broadcast_multiply_fusion.1, f32[768]{0:T(1024)S(1)} %copy-done.29, ...), kind=kOutput, calls=%fused_computation.105 | convolution fusion | flops 1215037440 | bytes 9063424 | tf_op jit(solution)/shard_map/dot_general | solution.py:244
  234.4 32.2 %attend_back.1 = bf16[2304,1024]{1,0:T(8,128)(2,1)} custom-call(s32[2,4]{1,0:T(2,128)} %pad_add_fusion.bounds, bf16[2304,1024]{1,0:T(8,128)(2,1)} %get-tuple-element.15.packed, bf16[768,1024]{1,0:T(8,128)(2,1)} %get-tuple-element.14.ctx, f32[12,1,1024]{2,1,0:T(1,128)} %get-tuple-element.16.lse, bf16[768,1024]{1,0:T(8,128)(2,1)} %fusion.58.gctx, s32[1,1024]{1,0:T(1,128)} %seg.3), custom_call_target="tpu_custom_call" | custom-call | tf_op jit(solution)/shard_map/attend_back/pallas_call | solution.py:214
  266.6 5.5 %fusion.61 = bf16[1,1024,768]{2,1,0:T(8,128)(2,1)} fusion(bf16[1024,768]{1,0:T(8,128)(2,1)} %copy-done.30, bf16[768,768]{1,0:T(8,128)(2,1)} %param.34, f32[768]{0:T(1024)S(1)} %copy-done.23, f32[768]{0:T(1024)S(1)} %copy-done.21, f32[1024]{0:T(1024)S(1)} %add_rsqrt_fusion, f32[1024,768]{1,0:T(8,128)} %copy-done.1, f32[1024]{0:T(1024)S(1)} %broadcast_multiply_fusion.4), kind=kOutput, calls=%fused_computation.106 | convolution fusion | flops 1212678144 | bytes 7485440 | tf_op jit(solution)/shard_map/dot_general | solution.py:234
  272.1 1.2 copy-done.10
  273.3 7.3 %fusion.57 = bf16[1,1024,768]{2,1,0:T(8,128)(2,1)} fusion(bf16[2304,1024]{1,0:T(8,128)(2,1)S(1)} %copy-done.7, bf16[768,2304]{1,0:T(8,128)(2,1)S(1)} %copy-done.8, f32[1024]{0:T(1024)S(1)} %broadcast_multiply_fusion, f32[1024,768]{1,0:T(8,128)S(1)} %copy-done.10, f32[1024]{0:T(1024)S(1)} %broadcast_multiply_fusion.5, ...), kind=kOutput, calls=%fused_computation.104 | convolution fusion | flops 3630956544 | bytes 16141312 | tf_op jit(solution)/shard_map/dot_general | solution.py:372
  280.5 57.2 %all-reduce.4.cloned.1.call-done = (f32[768,768]{1,0:T(8,128)}, f32[768,768]{1,0:T(8,128)}, f32[768,768]{1,0:T(8,128)}) async-done(((f32[768,768]{1,0:T(8,128)}, f32[768,768]{1,0:T(8,128)}, f32[768,768]{1,0:T(8,128)}), (f32[768,768]{1,0:T(8,128)}, f32[768,768]{1,0:T(8,128)}, f32[768,768]{1,0:T(8,128)})) %all-reduce.4.cloned.1.call-update) | async-done | bytes 7077904 | tf_op jit(solution)/shard_map/psum | solution.py:373
  337.7 3.4 copy.68
  341.1 1.4 copy.69
  342.5 1.1 copy-done.12
  343.6 1.4 copy.70
  (93 shorter events, 2.5 us)
Async XLA Ops:
  7.2 91.5 %copy-start = (bf16[768,768]{1,0:T(8,128)(2,1)S(1)}, bf16[768,768]{1,0:T(8,128)(2,1)}, u32[]{:S(2)}) copy-start(bf16[768,768]{1,0:T(8,128)(2,1)} %param.32) | copy-start | bytes 3538948
  7.2 36.8 %copy-start.16 = (bf16[1,1024,768]{2,1,0:T(8,128)(2,1)S(1)}, bf16[1,1024,768]{2,1,0:T(8,128)(2,1)}, u32[]{:S(2)}) copy-start(bf16[1,1024,768]{2,1,0:T(8,128)(2,1)} %param.18) | copy-start | bytes 4718596
  7.2 97.1 %all-gather.3.cloned.1.call-start = ((), (), s32[]{:S(2)}) async-start(), calls=%async_computation | async-start | bytes 1474560 | tf_op jit(solution)/shard_map/all_gather | solution.py:295
  7.9 108.2 %all-gather.5.cloned.1.call-start = ((), (), s32[]{:S(2)}) async-start(), calls=%async_computation.1 | async-start | bytes 1474560 | tf_op jit(solution)/shard_map/all_gather | solution.py:296
  8.7 329.1 %all-reduce.4.cloned.1.call-start = ((), (), s32[]{:S(2)}) async-start(), calls=%async_computation.2 | async-start | bytes 14155776 | tf_op jit(solution)/shard_map/psum | solution.py:373
  43.9 4.1 %slice-start.2 = ((s8[4718592]{0:T(1024)(128)(4,1)}), s8[4194304]{0:T(1024)(128)(4,1)S(1)}, s32[]{:S(2)}) async-start(s8[4718592]{0:T(1024)(128)(4,1)} %bitcast.99), calls=%async_computation.5 | async-start | bytes 8388608
  43.9 4.1 %slice-start.3 = ((s8[4718592]{0:T(1024)(128)(4,1)}), s8[524288]{0:T(1024)(128)(4,1)S(1)}, s32[]{:S(2)}) async-start(s8[4718592]{0:T(1024)(128)(4,1)} %bitcast.99), calls=%async_computation.6 | async-start | bytes 1048576
  47.5 6.0 %copy-start.9 = (f32[1024,768]{1,0:T(8,128)}, f32[1024,768]{1,0:T(8,128)S(1)}, u32[]{:S(2)}) copy-start(f32[1024,768]{1,0:T(8,128)S(1)} %get-tuple-element.46) | copy-start | bytes 9437188
  47.5 0.7 copy-start.28
  47.5 0.7 copy-start.29
  47.5 6.0 %slice-start = ((s8[4718592]{0:T(1024)(128)(4,1)}), s8[4194304]{0:T(1024)(128)(4,1)S(1)}, s32[]{:S(2)}) async-start(s8[4718592]{0:T(1024)(128)(4,1)} %bitcast.97), calls=%async_computation.3 | async-start | bytes 8388608
  48.2 5.3 %slice-start.1 = ((s8[4718592]{0:T(1024)(128)(4,1)}), s8[524288]{0:T(1024)(128)(4,1)S(1)}, s32[]{:S(2)}) async-start(s8[4718592]{0:T(1024)(128)(4,1)} %bitcast.97), calls=%async_computation.4 | async-start | bytes 1048576
  48.2 5.3 %copy-start.27 = (f32[3072]{0:T(1024)S(1)}, f32[3072]{0:T(1024)}, u32[]{:S(2)}) copy-start(f32[3072]{0:T(1024)} %param.24) | copy-start | bytes 36868
  53.5 43.5 %copy-start.32 = (f32[1024,3072]{1,0:T(8,128)}, f32[1024,3072]{1,0:T(8,128)S(1)}, u32[]{:S(2)}) copy-start(f32[1024,3072]{1,0:T(8,128)S(1)} %fusion.40) | copy-start | bytes 37748740
  97.0 1.7 copy-start.1
  97.0 0.7 copy-start.21
  97.0 0.8 copy-start.23
  98.7 7.3 %copy-start.17 = (bf16[1024,768]{1,0:T(8,128)(2,1)}, bf16[1024,768]{1,0:T(8,128)(2,1)S(1)}, u32[]{:S(2)}) copy-start(bf16[1024,768]{1,0:T(8,128)(2,1)S(1)} %fusion.37) | copy-start | bytes 4718596
  98.7 2.5 copy-start.14
  98.7 2.5 copy-start.26
  105.9 1.0 copy-start.19
  116.1 7.2 %copy-start.6 = (bf16[16,48,768]{2,0,1:T(8,128)(2,1)S(1)}, bf16[16,48,768]{2,0,1:T(8,128)(2,1)}, u32[]{:S(2)}) copy-start(bf16[16,48,768]{2,0,1:T(8,128)(2,1)} %all-gather.5.cloned.1.call-done) | copy-start | bytes 3538948
  123.3 5.8 %copy-start.3 = (f32[1024,768]{0,1:T(8,128)S(1)}, f32[1024,768]{0,1:T(8,128)}, u32[]{:S(2)}) copy-start(f32[1024,768]{0,1:T(8,128)} %get-tuple-element.49) | copy-start | bytes 9437188
  130.0 1.5 copy-start.24
  131.5 1.4 copy-start.31
  132.9 2.9 copy-start.4
  135.8 1.9 copy-start.11
  137.7 1.5 copy-start.20
  139.2 1.5 copy-start.18
  139.2 4.4 %copy-start.15 = (bf16[1,1024,768]{2,1,0:T(8,128)(2,1)S(1)}, bf16[1,1024,768]{2,1,0:T(8,128)(2,1)}, u32[]{:S(2)}) copy-start(bf16[1,1024,768]{2,1,0:T(8,128)(2,1)} %param.35) | copy-start | bytes 4718596
  140.7 2.9 copy-start.2
  140.7 3.8 %copy-start.5 = (f32[1024,768]{1,0:T(8,128)S(1)}, f32[1024,768]{1,0:T(8,128)}, u32[]{:S(2)}) copy-start(f32[1024,768]{1,0:T(8,128)} %fusion.46) | copy-start | bytes 9437188
  150.2 1.1 copy-start.30
  169.2 13.2 %copy-start.22 = (f32[1,1024]{1,0:T(1,128)S(1)}, f32[1,1024]{1,0:T(1,128)}, u32[]{:S(2)}) copy-start(f32[1,1024]{1,0:T(1,128)} %convert_element_type.101) | copy-start | bytes 12292
  169.2 59.2 %copy-start.25 = (bf16[768,768]{1,0:T(8,128)(2,1)S(1)}, bf16[768,768]{1,0:T(8,128)(2,1)}, u32[]{:S(2)}) copy-start(bf16[768,768]{1,0:T(8,128)(2,1)} %param.22) | copy-start | bytes 3538948
  266.6 5.5 %copy-start.7 = (bf16[2304,1024]{1,0:T(8,128)(2,1)S(1)}, bf16[2304,1024]{1,0:T(8,128)(2,1)}, u32[]{:S(2)}) copy-start(bf16[2304,1024]{1,0:T(8,128)(2,1)} %attend_back.1) | copy-start | bytes 14155780
  266.6 5.5 %copy-start.8 = (bf16[768,2304]{1,0:T(8,128)(2,1)S(1)}, bf16[768,2304]{1,0:T(8,128)(2,1)}, u32[]{:S(2)}) copy-start(bf16[768,2304]{1,0:T(8,128)(2,1)} %w.1) | copy-start | bytes 10616836
  266.6 6.7 %copy-start.10 = (f32[1024,768]{1,0:T(8,128)S(1)}, f32[1024,768]{1,0:T(8,128)}, u32[]{:S(2)}) copy-start(f32[1024,768]{1,0:T(8,128)} %copy-done.9) | copy-start | bytes 9437188
  337.7 3.4 copy-start.13
  341.1 2.5 copy-start.12
Sparse Core Ops, SparseCore 0:
  9.6 20.1 all-gather.2
  31.3 17.4 all-gather.4
  169.3 168.3 all-reduce.3
